TPU v7x, 128 devices: a whole 4x4x4 slice. The times are simulated.
128 devices in a mesh: rows: 16 (over z_lo, x, core), batch: 8 (over z_hi, y).
Axes of the slice: x: 4, y: 4, z: 4 (z_hi: 2, z_lo: 2; z = z_hi * 2 + z_lo), core: 2. Of those that a mesh axis runs over, the one named last changes fastest.
Arguments:
- bases: bfloat16 [49152, 2048], P('rows', 'batch'), may hold values from -30 to 30
- start: float32 [2048, 512], P('batch'), may hold values from -6 to 6
Outputs:
- modes: bfloat16 [49152, 512], P(('rows', 'batch'))
All inputs are finite; a program needn't handle non-finite values.
Results may differ from a plain program's by a relative error of at most 0.0041.
Values may be sent and summed in bfloat16 or wider, within the bound.
A program may use at most 128 MiB of HBM per device.

v0:
```python
import jax
import jax.numpy as jnp
from jax import lax
from jax.sharding import PartitionSpec as P

ITERS = 2


def inner_cols(left, right):
    return lax.dot_general(
        left, right, (((0,), (0,)), ((), ())), preferred_element_type=jnp.float32
    )


def on_device(bases, start):
    basis_width = bases.shape[1]
    group_count = lax.axis_size("batch")
    all_columns = basis_width * group_count
    energy = lax.psum(jnp.sum(jnp.square(bases.astype(jnp.float32))), ("rows", "batch"))
    diag_mean = energy / all_columns
    partial_value = inner_cols(bases, lax.all_gather(bases, "batch", axis=1, tiled=True))
    gram_rows = lax.psum(partial_value, "rows")
    q_own = start
    for iteration in range(ITERS):
        q_full = lax.all_gather(q_own, "batch", axis=0, tiled=True)
        lifted = jnp.dot(gram_rows, q_full, precision=lax.Precision.HIGHEST) / diag_mean + q_own
        local_correlation = lax.dot_general(
            lifted, lifted, (((0,), (0,)), ((), ())), precision=lax.Precision.HIGHEST
        )
        correlation = lax.psum(local_correlation, "batch")
        factor = jnp.linalg.cholesky(correlation)
        q_own = jax.scipy.linalg.solve_triangular(factor, lifted.T, lower=True).T
    q_low = q_own.astype(jnp.bfloat16)
    modes = lax.psum_scatter(
        jnp.dot(bases, q_low, preferred_element_type=jnp.float32),
        "batch",
        scatter_dimension=0,
        tiled=True,
    )
    return modes.astype(jnp.bfloat16)


def solution(mesh):
    in_specs = (P("rows", "batch"), P("batch", None))
    out_specs = P(("rows", "batch"), None)
    return jax.shard_map(
        on_device, mesh=mesh, in_specs=in_specs, out_specs=out_specs, check_vma=False
    )
```

profile of v0, /device:TPU:0, one launch (start us, length us, event | category | flops | bytes accessed | tf_op | source)
XLA Modules:
  0.0 1044.4 jit_solution(2930456255555356268)
XLA Ops:
  8.1 166.4 %all-gather.4.cloned.1.call-done = bf16[3072,2048]{1,0:T(8,128)(2,1)} async-done(((bf16[3072,256]{1,0:T(8,128)(2,1)}), bf16[3072,2048]{1,0:T(8,128)(2,1)}) %all-gather.4.cloned.1.call-update) | async-done | bytes 12582928 | tf_op jit(solution)/shard_map/all_gather | solution.py:21
  174.4 7.8 fusion.76
  182.3 1.4 multiply_reduce_fusion
  183.7 78.1 %psum.29 = f32[]{:T(128)} all-reduce(f32[]{:T(128)} %multiply_reduce_fusion), channel_id=1, replica_groups=mesh['rows'=16,'batch'=8] {'rows','batch'}, use_global_device_ids=true, to_apply=%region_2.0 | all-reduce | flops 1 | bytes 8 | tf_op jit(solution)/shard_map/psum | solution.py:19
  262.5 108.6 %all-reduce.5.cloned.1.call-done = f32[256,2048]{1,0:T(8,128)} async-done(((f32[256,2048]{1,0:T(8,128)}), f32[256,2048]{1,0:T(8,128)}) %all-reduce.5.cloned.1.call-update) | async-done | bytes 2097168 | tf_op jit(solution)/shard_map/psum | solution.py:22
  371.1 6.2 fusion
  377.3 2.1 fusion.77
  379.9 88.5 %all-reduce.7.cloned.1.call-done = f32[512,512]{0,1:T(8,128)} async-done(((f32[512,512]{0,1:T(8,128)}), f32[512,512]{0,1:T(8,128)}) %all-reduce.7.cloned.1.call-update) | async-done | bytes 1048592 | tf_op jit(solution)/shard_map/psum | solution.py:30
  468.5 2.7 copy.4
  471.2 1.4 fusion.2
  473.6 11.7 %cholesky.286 = f32[128,128]{1,0:T(8,128)S(1)} custom-call(f32[128,128]{1,0:T(8,128)S(1)} %cholesky.426), custom_call_target="Cholesky" | custom-call | tf_op jit(solution)/shard_map/jit(cholesky)/cholesky | solution.py:31
  485.4 9.8 custom-call.27
  497.8 11.7 %cholesky.305 = f32[128,128]{1,0:T(8,128)S(1)} custom-call(f32[128,128]{1,0:T(8,128)S(1)} %cholesky.430), custom_call_target="Cholesky" | custom-call | tf_op jit(solution)/shard_map/jit(cholesky)/cholesky | solution.py:31
  509.6 10.0 custom-call.28
  521.1 11.7 %cholesky.326 = f32[128,128]{1,0:T(8,128)S(1)} custom-call(f32[128,128]{1,0:T(8,128)S(1)} %cholesky.435), custom_call_target="Cholesky" | custom-call | tf_op jit(solution)/shard_map/jit(cholesky)/cholesky | solution.py:31
  533.6 9.8 custom-call.29
  544.8 11.7 %cholesky.343 = f32[128,128]{1,0:T(8,128)S(1)} custom-call(f32[128,128]{1,0:T(8,128)S(1)} %convolution_subtract_fusion.11), custom_call_target="Cholesky" | custom-call | tf_op jit(solution)/shard_map/jit(cholesky)/cholesky | solution.py:31
  561.8 11.7 %while.4 = (s32[]{:T(128)}, f32[512,512]{1,0:T(8,128)}, s32[4,2]{0,1:T(2,128)S(1)}, f32[4,128,128]{2,1,0:T(8,128)S(1)}, s32[]{:T(128)}) while((s32[]{:T(128)}, f32[512,512]{1,0:T(8,128)}, s32[4,2]{0,1:T(2,128)S(1)}, f32[4,128,128]{2,1,0:T(8,128)S(1)}, s32[]{:T(128)}) %tuple.52), condition=%wide.while_cond, body=%wide.while_body.sunk | while | flops 2 | bytes 131181 | solution.py:32
  562.5 2.3 bitcast_dynamic-update-slice_fusion.4
  565.4 2.3 bitcast_dynamic-update-slice_fusion.4
  568.4 2.3 bitcast_dynamic-update-slice_fusion.4
  571.3 2.2 bitcast_dynamic-update-slice_fusion.4
  573.5 39.3 %custom-call.30 = f32[4,128,128]{1,2,0:T(8,128)S(1)} custom-call(f32[4,128,128]{2,1,0:T(8,128)S(1)} %get-tuple-element.21), custom_call_target="InvertDiagBlocksLowerTriangular" | custom-call | tf_op jit(solution)/shard_map/jit(_solve_triangular)/triangular_solve | solution.py:32
  614.7 1.5 convolution_subtract_fusion.6
  616.5 1.7 convolution_subtract_fusion.5
  619.7 69.7 %all-gather.8.cloned.1.call-done = f32[2048,512]{1,0:T(8,128)} async-done(((f32[256,512]{1,0:T(8,128)}), f32[2048,512]{1,0:T(8,128)}) %all-gather.8.cloned.1.call-update) | async-done | bytes 4194320 | tf_op jit(solution)/shard_map/all_gather | solution.py:25
  689.4 6.3 bitcast_add_fusion.2
  695.7 2.1 fusion.3
  698.3 85.3 %all-reduce.9.cloned.1.call-done = f32[512,512]{0,1:T(8,128)} async-done(((f32[512,512]{0,1:T(8,128)}), f32[512,512]{0,1:T(8,128)}) %all-reduce.9.cloned.1.call-update) | async-done | bytes 1048592 | tf_op jit(solution)/shard_map/psum | solution.py:30
  783.7 2.7 copy.10
  786.4 1.4 fusion.1
  788.8 11.7 %cholesky.358 = f32[128,128]{1,0:T(8,128)S(1)} custom-call(f32[128,128]{1,0:T(8,128)S(1)} %cholesky.439), custom_call_target="Cholesky" | custom-call | tf_op jit(solution)/shard_map/jit(cholesky)/cholesky | solution.py:31
  800.7 9.8 custom-call.31
  813.1 11.7 %cholesky.377 = f32[128,128]{1,0:T(8,128)S(1)} custom-call(f32[128,128]{1,0:T(8,128)S(1)} %cholesky.443), custom_call_target="Cholesky" | custom-call | tf_op jit(solution)/shard_map/jit(cholesky)/cholesky | solution.py:31
  826.2 9.9 custom-call.32
  837.7 11.7 %cholesky.398 = f32[128,128]{1,0:T(8,128)S(1)} custom-call(f32[128,128]{1,0:T(8,128)S(1)} %cholesky.448), custom_call_target="Cholesky" | custom-call | tf_op jit(solution)/shard_map/jit(cholesky)/cholesky | solution.py:31
  850.1 9.8 custom-call.33
  861.3 11.7 %cholesky.415 = f32[128,128]{1,0:T(8,128)S(1)} custom-call(f32[128,128]{1,0:T(8,128)S(1)} %convolution_subtract_fusion.10), custom_call_target="Cholesky" | custom-call | tf_op jit(solution)/shard_map/jit(cholesky)/cholesky | solution.py:31
  877.7 11.7 %while.5 = (s32[]{:T(128)}, f32[512,512]{1,0:T(8,128)}, s32[4,2]{0,1:T(2,128)S(1)}, f32[4,128,128]{2,1,0:T(8,128)S(1)}, s32[]{:T(128)}) while((s32[]{:T(128)}, f32[512,512]{1,0:T(8,128)}, s32[4,2]{0,1:T(2,128)S(1)}, f32[4,128,128]{2,1,0:T(8,128)S(1)}, s32[]{:T(128)}) %tuple.72), condition=%wide.while_cond.clone, body=%wide.while_body.clone.sunk | while | flops 2 | bytes 131181 | solution.py:32
  878.4 2.3 bitcast_dynamic-update-slice_fusion.5
  881.4 2.3 bitcast_dynamic-update-slice_fusion.5
  884.3 2.3 bitcast_dynamic-update-slice_fusion.5
  887.2 2.2 bitcast_dynamic-update-slice_fusion.5
  889.4 39.3 %custom-call.34 = f32[4,128,128]{1,2,0:T(8,128)S(1)} custom-call(f32[4,128,128]{2,1,0:T(8,128)S(1)} %get-tuple-element.22), custom_call_target="InvertDiagBlocksLowerTriangular" | custom-call | tf_op jit(solution)/shard_map/jit(_solve_triangular)/triangular_solve | solution.py:32
  930.6 1.5 convolution_subtract_fusion.3
  932.5 1.8 convolution_subtract_fusion.2
  934.5 3.7 convolution_bitcast_fusion
  938.2 97.0 %reduce-scatter.2.cloned.1.call-done = f32[384,512]{0,1:T(8,128)} async-done(((f32[3072,512]{0,1:T(8,128)}), f32[384,512]{0,1:T(8,128)}) %reduce-scatter.2.cloned.1.call-update) | async-done | bytes 786448 | tf_op jit(solution)/shard_map/reduce_scatter | solution.py:34
  (100 shorter events, 37.1 us)
Async XLA Ops:
  6.5 167.9 %copy-start = (bf16[3072,256]{1,0:T(8,128)(2,1)S(1)}, bf16[3072,256]{1,0:T(8,128)(2,1)}, u32[]{:S(2)}) copy-start(bf16[3072,256]{1,0:T(8,128)(2,1)} %param.5) | copy-start | bytes 4718596
  6.5 167.9 %all-gather.4.cloned.1.call-start = ((), (), s32[]{:S(2)}) async-start(), calls=%async_computation.1 | async-start | bytes 14155776 | tf_op jit(solution)/shard_map/all_gather | solution.py:21
  7.3 255.2 %all-gather.6.cloned.1.call-start = ((), (), s32[]{:S(2)}) async-start(), calls=%async_computation.3 | async-start | bytes 4718592 | tf_op jit(solution)/shard_map/all_gather | solution.py:25
  8.0 363.1 %all-reduce.5.cloned.1.call-start = ((), (), s32[]{:S(2)}) async-start(), calls=%async_computation.2 | async-start | bytes 4194304 | tf_op jit(solution)/shard_map/psum | solution.py:22
  182.2 188.8 %copy-start.5 = (f32[256,512]{1,0:T(8,128)S(1)}, f32[256,512]{1,0:T(8,128)}, u32[]{:S(2)}) copy-start(f32[256,512]{1,0:T(8,128)} %param.6) | copy-start | bytes 1572868
  182.3 286.2 %all-reduce.7.cloned.1.call-start = ((), (), s32[]{:S(2)}) async-start(), calls=%async_computation.4 | async-start | bytes 2097152 | tf_op jit(solution)/shard_map/psum | solution.py:30
  379.4 310.0 %all-gather.8.cloned.1.call-start = ((), (), s32[]{:S(2)}) async-start(), calls=%async_computation.5 | async-start | bytes 4718592 | tf_op jit(solution)/shard_map/all_gather | solution.py:25
  468.5 2.7 copy-start.1
  472.6 1.0 copy-start.4
  619.7 164.0 %all-reduce.9.cloned.1.call-start = ((), (), s32[]{:S(2)}) async-start(), calls=%async_computation.6 | async-start | bytes 2097152 | tf_op jit(solution)/shard_map/psum | solution.py:30
  697.9 337.3 %reduce-scatter.2.cloned.1.call-start = ((), (), s32[]{:S(2)}) async-start(), calls=%async_computation.7 | async-start | bytes 7077888 | tf_op jit(solution)/shard_map/reduce_scatter | solution.py:34
  783.7 2.7 copy-start.2
  787.8 1.0 copy-start.3
Sparse Core Ops, SparseCore 0:
  9.5 164.8 all-gather.3
  176.7 70.8 all-gather.5
  250.1 120.8 all-reduce.4
  379.5 88.8 all-reduce.6
  619.8 69.5 all-gather.7
  698.0 85.6 all-reduce.8
  938.4 96.8 reduce-scatter.1
where the time goes:
time: 1050 us; the launch traced here: 1040 us
  waiting for transfers between devices  617 us (59%)
  other arithmetic  246 us (23%)
  blocking collectives  78.1 us (7%)
  matrix products  50.6 us (5%)
  local copies, waits for them, and re-layouts  32.1 us (3%)
  between operations  19.8 us (2%)
    psum x2, waiting for transfers between devices, on_device(): correlation = lax.psum(local_correlation, 'batch')  174 us
    all_gather x1, waiting for transfers between devices, on_device(): lax.all_gather(bases, 'batch', axis=1, tiled=True)  166 us
    another operation x29, other arithmetic, on_device(): factor = jnp.linalg.cholesky(correlation)  158 us
    psum x1, waiting for transfers between devices, on_device(): gram_rows = lax.psum(partial_value, 'rows')  109 us
    reduce_scatter x1, waiting for transfers between devices, on_device(): lax.psum_scatter(jnp.dot(bases, q_low, preferred_element_type=jnp.float32...  97 us
    another operation x5, other arithmetic, on_device(): q_own = jax.scipy.linalg.solve_triangular(factor, lifted.T, lower=True).T  81.3 us
    psum x1, blocking collectives, on_device(): lax.psum(jnp.sum(jnp.square(bases.astype(jnp.float32))), ('rows', 'batch'))  78.1 us
    all_gather x2, waiting for transfers between devices, on_device(): q_full = lax.all_gather(q_own, 'batch', axis=0, tiled=True)  69.7 us
  transfers between devices with their start and end apart: 7, of which 6 were waited for; matrix products, arithmetic and copies ran while one was open for 1% of the time, Pallas kernels for 0%

commit v1 on v0

--- a/solution.py
+++ b/solution.py
@@ -22,7 +22,9 @@
     gram_rows = lax.psum(partial_value, "rows")
     q_own = start
     for iteration in range(ITERS):
-        q_full = lax.all_gather(q_own, "batch", axis=0, tiled=True)
+        q_full = jnp.concatenate(
+            lax.all_to_all(jnp.stack([q_own] * lax.axis_size("batch")), "batch", 0, 0), axis=0
+        )
         lifted = jnp.dot(gram_rows, q_full, precision=lax.Precision.HIGHEST) / diag_mean + q_own
         local_correlation = lax.dot_general(
             lifted, lifted, (((0,), (0,)), ((), ())), precision=lax.Precision.HIGHEST

time: 1050 us -> 1010 us (0.962)
  waiting for transfers between devices: 617 us -> 532 us
  blocking collectives: 78.1 us -> 114 us
    all_gather x2 -> x0, waiting for transfers between devices: 69.7 us -> none  [on_device(): q_full = lax.all_gather(q_own, 'batch', axis=0, tiled=True)]
    psum x1, waiting for transfers between devices: 109 us -> 55.4 us  [on_device(): gram_rows = lax.psum(partial_value, 'rows')]
    all_to_all x0 -> x1, blocking collectives: none -> 48.7 us  [on_device(): lax.all_to_all(jnp.stack([q_own] * lax.axis_size('batch')), 'batch', 0, 0)]
    all_gather x1, waiting for transfers between devices: 166 us -> 205 us  [on_device(): lax.all_gather(bases, 'batch', axis=1, tiled=True)]
    psum x1, blocking collectives: 78.1 us -> 65 us  [on_device(): lax.psum(jnp.sum(jnp.square(bases.astype(jnp.float32))), ('rows', 'batch'))]
  transfers between devices with their start and end apart: 7 -> 6, of which waited for: 6 -> 5; matrix products, arithmetic and copies ran while one was open for 1% -> 1% of each run, Pallas kernels for 0% -> 0%
where the time goes in v1:
time: 1010 us; the launch traced here: 1000 us
  waiting for transfers between devices  532 us (53%)
  other arithmetic  245 us (24%)
  blocking collectives  114 us (11%)
  matrix products  49.8 us (5%)
  local copies, waits for them, and re-layouts  33.2 us (3%)
  between operations  19.4 us (2%)
    all_gather x1, waiting for transfers between devices, on_device(): lax.all_gather(bases, 'batch', axis=1, tiled=True)  205 us
    psum x2, waiting for transfers between devices, on_device(): correlation = lax.psum(local_correlation, 'batch')  174 us
    another operation x29, other arithmetic, on_device(): factor = jnp.linalg.cholesky(correlation)  158 us
    reduce_scatter x1, waiting for transfers between devices, on_device(): lax.psum_scatter(jnp.dot(bases, q_low, preferred_element_type=jnp.float32...  97 us
    another operation x5, other arithmetic, on_device(): q_own = jax.scipy.linalg.solve_triangular(factor, lifted.T, lower=True).T  81.3 us
    psum x1, blocking collectives, on_device(): lax.psum(jnp.sum(jnp.square(bases.astype(jnp.float32))), ('rows', 'batch'))  65 us
    psum x1, waiting for transfers between devices, on_device(): gram_rows = lax.psum(partial_value, 'rows')  55.4 us
    all_to_all x1, blocking collectives, on_device(): lax.all_to_all(jnp.stack([q_own] * lax.axis_size('batch')), 'batch', 0, 0)  48.7 us
  transfers between devices with their start and end apart: 6, of which 5 were waited for; matrix products, arithmetic and copies ran while one was open for 1% of the time, Pallas kernels for 0%

profile of v1, /device:TPU:0, one launch (start us, length us, event | category | flops | bytes accessed | tf_op | source)
XLA Modules:
  0.0 1001.9 jit_solution(10805643475178409122)
XLA Ops:
  7.3 3.5 stack.4
  10.8 8.0 all-to-all-start
  18.8 204.9 %all-gather.2.cloned.1.call-done = bf16[3072,2048]{1,0:T(8,128)(2,1)} async-done(((bf16[3072,256]{1,0:T(8,128)(2,1)}), bf16[3072,2048]{1,0:T(8,128)(2,1)}) %all-gather.2.cloned.1.call-update) | async-done | bytes 12582928 | tf_op jit(solution)/shard_map/all_gather | solution.py:21
  223.7 7.8 fusion.76
  233.0 65.0 %psum.29 = f32[]{:T(128)} all-reduce(f32[]{:T(128)} %multiply_reduce_fusion), channel_id=1, replica_groups=mesh['rows'=16,'batch'=8] {'rows','batch'}, use_global_device_ids=true, to_apply=%region_2.0 | all-reduce | flops 1 | bytes 8 | tf_op jit(solution)/shard_map/psum | solution.py:19
  298.7 55.4 %all-reduce.5.cloned.1.call-done = f32[256,2048]{1,0:T(8,128)} async-done(((f32[256,2048]{1,0:T(8,128)}), f32[256,2048]{1,0:T(8,128)}) %all-reduce.5.cloned.1.call-update) | async-done | bytes 2097168 | tf_op jit(solution)/shard_map/psum | solution.py:22
  354.0 6.2 fusion
  360.3 2.0 fusion.77
  362.9 88.5 %all-reduce.7.cloned.1.call-done = f32[512,512]{0,1:T(8,128)} async-done(((f32[512,512]{0,1:T(8,128)}), f32[512,512]{0,1:T(8,128)}) %all-reduce.7.cloned.1.call-update) | async-done | bytes 1048592 | tf_op jit(solution)/shard_map/psum | solution.py:32
  451.4 1.6 copy.4
  455.4 11.7 %cholesky.286 = f32[128,128]{1,0:T(8,128)S(1)} custom-call(f32[128,128]{1,0:T(8,128)S(1)} %cholesky.426), custom_call_target="Cholesky" | custom-call | tf_op jit(solution)/shard_map/jit(cholesky)/cholesky | solution.py:33
  467.1 9.8 custom-call.27
  479.6 11.7 %cholesky.305 = f32[128,128]{1,0:T(8,128)S(1)} custom-call(f32[128,128]{1,0:T(8,128)S(1)} %cholesky.430), custom_call_target="Cholesky" | custom-call | tf_op jit(solution)/shard_map/jit(cholesky)/cholesky | solution.py:33
  491.4 10.0 custom-call.28
  502.9 11.7 %cholesky.326 = f32[128,128]{1,0:T(8,128)S(1)} custom-call(f32[128,128]{1,0:T(8,128)S(1)} %cholesky.435), custom_call_target="Cholesky" | custom-call | tf_op jit(solution)/shard_map/jit(cholesky)/cholesky | solution.py:33
  515.2 9.8 custom-call.29
  526.5 11.7 %cholesky.343 = f32[128,128]{1,0:T(8,128)S(1)} custom-call(f32[128,128]{1,0:T(8,128)S(1)} %convolution_subtract_fusion.11), custom_call_target="Cholesky" | custom-call | tf_op jit(solution)/shard_map/jit(cholesky)/cholesky | solution.py:33
  543.4 11.1 %while.4 = (s32[]{:T(128)}, f32[512,512]{1,0:T(8,128)}, s32[4,2]{0,1:T(2,128)S(1)}, f32[4,128,128]{2,1,0:T(8,128)S(1)}, s32[]{:T(128)}) while((s32[]{:T(128)}, f32[512,512]{1,0:T(8,128)}, s32[4,2]{0,1:T(2,128)S(1)}, f32[4,128,128]{2,1,0:T(8,128)S(1)}, s32[]{:T(128)}) %tuple.52), condition=%wide.while_cond, body=%wide.while_body.sunk | while | flops 2 | bytes 131181 | solution.py:34
  544.0 2.2 bitcast_dynamic-update-slice_fusion.4
  546.8 2.2 bitcast_dynamic-update-slice_fusion.4
  549.6 2.2 bitcast_dynamic-update-slice_fusion.4
  552.3 2.1 bitcast_dynamic-update-slice_fusion.4
  554.4 39.3 %custom-call.30 = f32[4,128,128]{1,2,0:T(8,128)S(1)} custom-call(f32[4,128,128]{2,1,0:T(8,128)S(1)} %get-tuple-element.21), custom_call_target="InvertDiagBlocksLowerTriangular" | custom-call | tf_op jit(solution)/shard_map/jit(_solve_triangular)/triangular_solve | solution.py:34
  595.6 1.5 convolution_subtract_fusion.6
  597.5 1.7 convolution_subtract_fusion.5
  600.4 48.7 %all_to_all.10 = f32[8,256,512]{2,1,0:T(8,128)S(1)} all-to-all(f32[8,256,512]{2,1,0:T(8,128)S(1)} %stack.5), channel_id=1, replica_groups=mesh['rows'=16,'batch'=8] {'batch'}, dimensions={0} | all-to-all | bytes 8388608 | tf_op jit(solution)/shard_map/all_to_all | solution.py:26
  649.1 4.5 bitcast_add_fusion.2
  653.6 2.1 fusion.3
  656.2 85.3 %all-reduce.9.cloned.1.call-done = f32[512,512]{0,1:T(8,128)} async-done(((f32[512,512]{0,1:T(8,128)}), f32[512,512]{0,1:T(8,128)}) %all-reduce.9.cloned.1.call-update) | async-done | bytes 1048592 | tf_op jit(solution)/shard_map/psum | solution.py:32
  741.5 1.6 copy.10
  743.1 1.4 fusion.1
  745.6 11.7 %cholesky.358 = f32[128,128]{1,0:T(8,128)S(1)} custom-call(f32[128,128]{1,0:T(8,128)S(1)} %cholesky.439), custom_call_target="Cholesky" | custom-call | tf_op jit(solution)/shard_map/jit(cholesky)/cholesky | solution.py:33
  757.4 9.8 custom-call.31
  769.8 11.7 %cholesky.377 = f32[128,128]{1,0:T(8,128)S(1)} custom-call(f32[128,128]{1,0:T(8,128)S(1)} %cholesky.443), custom_call_target="Cholesky" | custom-call | tf_op jit(solution)/shard_map/jit(cholesky)/cholesky | solution.py:33
  782.9 10.0 custom-call.32
  794.4 11.7 %cholesky.398 = f32[128,128]{1,0:T(8,128)S(1)} custom-call(f32[128,128]{1,0:T(8,128)S(1)} %cholesky.448), custom_call_target="Cholesky" | custom-call | tf_op jit(solution)/shard_map/jit(cholesky)/cholesky | solution.py:33
  806.8 9.8 custom-call.33
  818.1 11.7 %cholesky.415 = f32[128,128]{1,0:T(8,128)S(1)} custom-call(f32[128,128]{1,0:T(8,128)S(1)} %convolution_subtract_fusion.10), custom_call_target="Cholesky" | custom-call | tf_op jit(solution)/shard_map/jit(cholesky)/cholesky | solution.py:33
  834.4 11.7 %while.5 = (s32[]{:T(128)}, f32[512,512]{1,0:T(8,128)}, s32[4,2]{0,1:T(2,128)S(1)}, f32[4,128,128]{2,1,0:T(8,128)S(1)}, s32[]{:T(128)}) while((s32[]{:T(128)}, f32[512,512]{1,0:T(8,128)}, s32[4,2]{0,1:T(2,128)S(1)}, f32[4,128,128]{2,1,0:T(8,128)S(1)}, s32[]{:T(128)}) %tuple.68), condition=%wide.while_cond.clone, body=%wide.while_body.clone.sunk | while | flops 2 | bytes 131181 | solution.py:34
  835.1 2.3 bitcast_dynamic-update-slice_fusion.5
  838.0 2.3 bitcast_dynamic-update-slice_fusion.5
  840.9 2.3 bitcast_dynamic-update-slice_fusion.5
  843.9 2.2 bitcast_dynamic-update-slice_fusion.5
  846.1 39.3 %custom-call.34 = f32[4,128,128]{1,2,0:T(8,128)S(1)} custom-call(f32[4,128,128]{2,1,0:T(8,128)S(1)} %get-tuple-element.22), custom_call_target="InvertDiagBlocksLowerTriangular" | custom-call | tf_op jit(solution)/shard_map/jit(_solve_triangular)/triangular_solve | solution.py:34
  888.3 1.6 convolution_subtract_fusion.3
  890.2 1.8 convolution_subtract_fusion.2
  892.3 3.7 convolution_bitcast_fusion
  896.0 97.0 %reduce-scatter.2.cloned.1.call-done = f32[384,512]{0,1:T(8,128)} async-done(((f32[3072,512]{0,1:T(8,128)}), f32[384,512]{0,1:T(8,128)}) %reduce-scatter.2.cloned.1.call-update) | async-done | bytes 786448 | tf_op jit(solution)/shard_map/reduce_scatter | solution.py:36
  (97 shorter events, 39.5 us)
Async XLA Ops:
  6.5 217.2 %all-gather.2.cloned.1.call-start = ((), (), s32[]{:S(2)}) async-start(), calls=%async_computation.3 | async-start | bytes 14155776 | tf_op jit(solution)/shard_map/all_gather | solution.py:21
  10.8 212.9 %copy-start = (bf16[3072,256]{1,0:T(8,128)(2,1)S(1)}, bf16[3072,256]{1,0:T(8,128)(2,1)}, u32[]{:S(2)}) copy-start(bf16[3072,256]{1,0:T(8,128)(2,1)} %param.5) | copy-start | bytes 4718596
  10.8 287.9 %all-to-all-start = ((f32[8,256,512]{2,1,0:T(8,128)}), f32[8,256,512]{2,1,0:T(8,128)}, u32[]{:S(2)}, u32[]{:S(2)}) async-start(f32[8,256,512]{2,1,0:T(8,128)} %stack.4), calls=%async_computation | async-start | bytes 8388608 | tf_op jit(solution)/shard_map/all_to_all | solution.py:26
  18.8 335.2 %all-reduce.5.cloned.1.call-start = ((), (), s32[]{:S(2)}) async-start(), calls=%async_computation.4 | async-start | bytes 4194304 | tf_op jit(solution)/shard_map/psum | solution.py:22
  231.5 122.5 %copy-start.4 = (f32[256,512]{1,0:T(8,128)S(1)}, f32[256,512]{1,0:T(8,128)}, u32[]{:S(2)}) copy-start(f32[256,512]{1,0:T(8,128)} %param.6) | copy-start | bytes 1572868
  231.5 219.9 %all-reduce.7.cloned.1.call-start = ((), (), s32[]{:S(2)}) async-start(), calls=%async_computation.5 | async-start | bytes 2097152 | tf_op jit(solution)/shard_map/psum | solution.py:32
  362.3 379.2 %all-reduce.9.cloned.1.call-start = ((), (), s32[]{:S(2)}) async-start(), calls=%async_computation.6 | async-start | bytes 2097152 | tf_op jit(solution)/shard_map/psum | solution.py:32
  454.4 1.0 copy-start.3
  600.4 48.7 %copy-start.1 = (f32[256,2048]{1,0:T(8,128)S(1)}, f32[256,2048]{1,0:T(8,128)}, u32[]{:S(2)}) copy-start(f32[256,2048]{1,0:T(8,128)} %all-reduce.5.cloned.1.call-done) | copy-start | bytes 6291460
  655.7 337.3 %reduce-scatter.2.cloned.1.call-start = ((), (), s32[]{:S(2)}) async-start(), calls=%async_computation.7 | async-start | bytes 7077888 | tf_op jit(solution)/shard_map/reduce_scatter | solution.py:36
  744.5 1.0 copy-start.2
Sparse Core Ops, SparseCore 0:
  9.5 214.1 all-gather.1
  231.6 122.3 all-reduce.4
  362.4 88.8 all-reduce.6
  655.9 85.6 all-reduce.8
  896.1 96.8 reduce-scatter.1
